TPU v7x, 32 devices: a whole 2x2x4 slice. The times are simulated.
32 devices in a mesh: rep: 4 (over y, x), fsdp: 8 (over z, core).
Axes of the slice: x: 2, y: 2, z: 4, core: 2. Of those that a mesh axis runs over, the one named last changes fastest.
Arguments:
- tokens: float32 [4096, 1024], P(('rep', 'fsdp')), may hold values from -6 to 6
- segment_ids: int32 [4096], replicated, may hold values from 0 to 7, never falling along the last dimension, each value on 1 to 1024 neighbouring positions
- cotangent: float32 [4096, 1024], P(('rep', 'fsdp')), may hold values from -6 to 6
- w_qkv: bfloat16 [1024, 2048], P('fsdp'), may hold values from -0.1875 to 0.1875
- w_out: bfloat16 [1024, 1024], P('fsdp'), may hold values from -0.75 to 0.75
- w_gate_up: bfloat16 [1024, 9216], P('fsdp'), may hold values from -0.1875 to 0.1875
- w_down: bfloat16 [4608, 1024], P('fsdp'), may hold values from -0.09375 to 0.09375
- g_attn: bfloat16 [1024], P('fsdp'), may hold values from 0.099609375 to 1.8984375
- g_query: bfloat16 [64], P('fsdp'), may hold values from 0.099609375 to 1.8984375
- g_key: bfloat16 [64], P('fsdp'), may hold values from 0.099609375 to 1.8984375
- g_ffn: bfloat16 [1024], P('fsdp'), may hold values from 0.099609375 to 1.8984375
Outputs:
- output: float32 [4096, 1024], P(('rep', 'fsdp'))
- grad_tokens: float32 [4096, 1024], P(('rep', 'fsdp'))
- grad_w_qkv: float32 [1024, 2048], P('fsdp')
- grad_w_out: float32 [1024, 1024], P('fsdp')
- grad_w_gate_up: float32 [1024, 9216], P('fsdp')
- grad_w_down: float32 [4608, 1024], P('fsdp')
- grad_g_attn: float32 [1024], P('fsdp')
- grad_g_query: float32 [64], P('fsdp')
- grad_g_key: float32 [64], P('fsdp')
- grad_g_ffn: float32 [1024], P('fsdp')
Inputs may be any that keep to these rules, and one draw needn't show every extreme that they name: `segment_ids`: segment numbers never fall along the tokens; a segment holds 1 to 1024 tokens and one holds exactly 1024.
All inputs are finite; a program needn't handle non-finite values.
Results may differ from a plain program's by a relative error of at most 0.024.
Values may be sent and summed in bfloat16 or wider, within the bound.
A program may use at most 192 MiB of HBM per device.

v0:
```python
import jax
import jax.numpy as jnp
from jax import lax
from jax.sharding import PartitionSpec as P

QUERY_HEADS = 16
KEY_VALUE_HEADS = 8
HEAD_SIZE = 64
FF = 4608
NORM_EPS = 1e-05
ROPE_BASE = 1000000.0
MASK_FILL = -1e30


def rms_forward(values, gain_vec):
    inv_rms = lax.rsqrt(jnp.mean(values * values, axis=-1, keepdims=True) + NORM_EPS)
    return (values * inv_rms * gain_vec, inv_rms)


def root_mean_square_reverse(values, inv_rms, gain_vec, grad_out):
    weighted = grad_out * gain_vec
    grad_values = inv_rms * weighted - values * inv_rms**3 * jnp.mean(
        weighted * values, axis=-1, keepdims=True
    )
    grad_gain = jnp.sum((grad_out * values * inv_rms).reshape(-1, values.shape[-1]), axis=0)
    return (grad_values, grad_gain)


def rope_tables(positions, head_width):
    half_width = head_width // 2
    freqs_base = ROPE_BASE ** (-2.0 * jnp.arange(half_width, dtype=jnp.float32) / head_width)
    angles = positions.astype(jnp.float32)[:, None] * freqs_base[None, :]
    return (jnp.cos(angles)[:, None, :], jnp.sin(angles)[:, None, :])


def rotary_embed_apply(values, rotary_cosine, rotary_sine):
    half_width = values.shape[-1] // 2
    first_half = values[..., :half_width]
    second_half = values[..., half_width:]
    return jnp.concatenate(
        [
            first_half * rotary_cosine - second_half * rotary_sine,
            second_half * rotary_cosine + first_half * rotary_sine,
        ],
        axis=-1,
    )


def rotary_embed_invert(grad_out, rotary_cosine, rotary_sine):
    half_width = grad_out.shape[-1] // 2
    first_half = grad_out[..., :half_width]
    second_half = grad_out[..., half_width:]
    return jnp.concatenate(
        [
            first_half * rotary_cosine + second_half * rotary_sine,
            second_half * rotary_cosine - first_half * rotary_sine,
        ],
        axis=-1,
    )


def score_block(query_lowprec, key_lowprec, attention_mask_matrix):
    scale_dot = query_lowprec.shape[-1] ** (-0.5)
    scores = (
        jnp.einsum("qkgd,tkd->kgqt", query_lowprec, key_lowprec, preferred_element_type=jnp.float32)
        * scale_dot
    )
    return jnp.where(attention_mask_matrix, scores, MASK_FILL)


def attend_forward(query_lowprec, key_lowprec, value_lowprec, attention_mask_matrix):
    scores = score_block(query_lowprec, key_lowprec, attention_mask_matrix)
    top_score = jnp.max(scores, axis=-1, keepdims=True)
    expo_terms = jnp.where(attention_mask_matrix, jnp.exp(scores - top_score), 0.0)
    row_total = jnp.sum(expo_terms, axis=-1, keepdims=True)
    probs = (expo_terms / row_total).astype(jnp.bfloat16)
    mixed = jnp.einsum("kgqt,tkd->qkgd", probs, value_lowprec, preferred_element_type=jnp.float32)
    return (mixed.astype(jnp.bfloat16), top_score + jnp.log(row_total))


def attention_reverse_pass(
    query_lowprec,
    key_lowprec,
    value_lowprec,
    attention_mask_matrix,
    attention_lowprec,
    log_partition_sum,
    grad_attn,
):
    scale_dot = query_lowprec.shape[-1] ** (-0.5)
    scores = score_block(query_lowprec, key_lowprec, attention_mask_matrix)
    probs_again = jnp.where(attention_mask_matrix, jnp.exp(scores - log_partition_sum), 0.0)
    probs_low = probs_again.astype(jnp.bfloat16)
    value_gradient_rows = jnp.einsum(
        "kgqt,qkgd->tkd", probs_low, grad_attn, preferred_element_type=jnp.float32
    )
    d_probs = jnp.einsum(
        "qkgd,tkd->kgqt", grad_attn, value_lowprec, preferred_element_type=jnp.float32
    )
    delta_rows = jnp.sum(
        grad_attn.astype(jnp.float32) * attention_lowprec.astype(jnp.float32), axis=-1
    )
    delta_rows = jnp.transpose(delta_rows, (1, 2, 0))[..., None]
    d_score = (probs_again * (d_probs - delta_rows) * scale_dot).astype(jnp.bfloat16)
    grad_query = jnp.einsum(
        "kgqt,tkd->qkgd", d_score, key_lowprec, preferred_element_type=jnp.float32
    )
    grad_key = jnp.einsum(
        "kgqt,qkgd->tkd", d_score, query_lowprec, preferred_element_type=jnp.float32
    )
    return (grad_query, grad_key, value_gradient_rows)


def tdot(left_arr, right_arr):
    return lax.dot_general(
        left_arr, right_arr, (((0,), (0,)), ((), ())), preferred_element_type=jnp.float32
    )


def transposed_product(left_arr, right_arr):
    return lax.dot_general(
        left_arr, right_arr, (((1,), (1,)), ((), ())), preferred_element_type=jnp.float32
    )


def body(
    tokens, segment_ids, cotangent, w_qkv, w_out, w_gate_up, w_down, g_attn, g_query, g_key, g_ffn
):
    local_rows = tokens.shape[0]
    cluster_size = QUERY_HEADS // KEY_VALUE_HEADS
    seq_devices = lax.axis_size("fsdp")
    cluster_rows = seq_devices * local_rows
    member = lax.axis_index("fsdp")
    own_group = member * local_rows
    group_start = lax.axis_index("rep") * cluster_rows
    own_global = group_start + own_group
    key_value_width = KEY_VALUE_HEADS * HEAD_SIZE
    shards = (w_qkv, w_out, w_gate_up, w_down, g_attn, g_query, g_key, g_ffn)
    collected_rows = (
        lax.all_gather(shards[0], "fsdp", axis=0, tiled=True),
        lax.all_gather(shards[1], "fsdp", axis=0, tiled=True),
        lax.all_gather(shards[2], "fsdp", axis=0, tiled=True),
        lax.all_gather(shards[3], "fsdp", axis=0, tiled=True),
        lax.all_gather(shards[4], "fsdp", axis=0, tiled=True),
        lax.all_gather(shards[5], "fsdp", axis=0, tiled=True),
        lax.all_gather(shards[6], "fsdp", axis=0, tiled=True),
        lax.all_gather(shards[7], "fsdp", axis=0, tiled=True),
    )
    gain_sequence = [gain_arr.astype(jnp.float32) for gain_arr in collected_rows[4:]]
    query_seg = lax.dynamic_slice_in_dim(segment_ids, own_global, local_rows)
    key_seg = lax.dynamic_slice_in_dim(segment_ids, group_start, cluster_rows)
    query_pos = own_group + jnp.arange(local_rows, dtype=jnp.int32)
    key_pos = jnp.arange(cluster_rows, dtype=jnp.int32)
    attention_mask_matrix = (key_pos[None, :] <= query_pos[:, None]) & (
        query_seg[:, None] == key_seg[None, :]
    )
    rotary_cosine, rotary_sine = rope_tables(query_pos, HEAD_SIZE)
    normed_f, inv_in = rms_forward(tokens, gain_sequence[0])
    normed_in = normed_f.astype(jnp.bfloat16)
    projection_output = jnp.dot(normed_in, collected_rows[0], preferred_element_type=jnp.float32)
    query_raw = projection_output[:, : QUERY_HEADS * HEAD_SIZE].reshape(
        local_rows, QUERY_HEADS, HEAD_SIZE
    )
    key_unrotated = projection_output[
        :, QUERY_HEADS * HEAD_SIZE : (QUERY_HEADS + KEY_VALUE_HEADS) * HEAD_SIZE
    ].reshape(local_rows, KEY_VALUE_HEADS, HEAD_SIZE)
    value_lowprec = projection_output[:, (QUERY_HEADS + KEY_VALUE_HEADS) * HEAD_SIZE :].astype(
        jnp.bfloat16
    )
    query_norm_output, inv_query = rms_forward(query_raw, gain_sequence[1])
    key_norm, key_inverse_norm = rms_forward(key_unrotated, gain_sequence[2])
    query_lowprec = (
        rotary_embed_apply(query_norm_output, rotary_cosine, rotary_sine)
        .astype(jnp.bfloat16)
        .reshape(local_rows, KEY_VALUE_HEADS, cluster_size, HEAD_SIZE)
    )
    key_lowprec = rotary_embed_apply(key_norm, rotary_cosine, rotary_sine).astype(jnp.bfloat16)
    kv_pair = jnp.stack([key_lowprec.reshape(local_rows, key_value_width), value_lowprec])
    key_value_span = lax.all_gather(kv_pair, "fsdp", axis=1, tiled=True)
    span_keys = key_value_span[0].reshape(cluster_rows, KEY_VALUE_HEADS, HEAD_SIZE)
    span_values = key_value_span[1].reshape(cluster_rows, KEY_VALUE_HEADS, HEAD_SIZE)
    attention_lowprec, log_partition_sum = attend_forward(
        query_lowprec, span_keys, span_values, attention_mask_matrix
    )
    attn_flat = attention_lowprec.reshape(local_rows, QUERY_HEADS * HEAD_SIZE)
    mid_stream = tokens + jnp.dot(attn_flat, collected_rows[1], preferred_element_type=jnp.float32)
    normed_g, inv_mid = rms_forward(mid_stream, gain_sequence[3])
    normed_mid = normed_g.astype(jnp.bfloat16)
    gate_up = jnp.dot(normed_mid, collected_rows[2], preferred_element_type=jnp.float32)
    gate_part = gate_up[:, :FF]
    up_part = gate_up[:, FF:]
    sigmoid_gate = jax.nn.sigmoid(gate_part)
    hidden = (gate_part * sigmoid_gate * up_part).astype(jnp.bfloat16)
    output = mid_stream + jnp.dot(hidden, collected_rows[3], preferred_element_type=jnp.float32)
    cot_low = cotangent.astype(jnp.bfloat16)
    grad_down = tdot(hidden, cot_low)
    d_hidden = transposed_product(cot_low, collected_rows[3])
    d_gate = d_hidden * up_part * sigmoid_gate * (1.0 + gate_part * (1.0 - sigmoid_gate))
    d_up = d_hidden * gate_part * sigmoid_gate
    d_gate_up = jnp.concatenate([d_gate, d_up], axis=1).astype(jnp.bfloat16)
    grad_gate_up = tdot(normed_mid, d_gate_up)
    d_normed_mid = transposed_product(d_gate_up, collected_rows[2])
    back_mid, grad_ffn_gain = root_mean_square_reverse(
        mid_stream, inv_mid, gain_sequence[3], d_normed_mid
    )
    d_mid = cotangent + back_mid
    middle_cotangent_lowprec = d_mid.astype(jnp.bfloat16)
    grad_out_proj = tdot(attn_flat, middle_cotangent_lowprec)
    attention_cotangent = (
        transposed_product(middle_cotangent_lowprec, collected_rows[1])
        .astype(jnp.bfloat16)
        .reshape(local_rows, KEY_VALUE_HEADS, cluster_size, HEAD_SIZE)
    )
    query_lowprec_gradient, grad_kwin, grad_vwin = attention_reverse_pass(
        query_lowprec,
        span_keys,
        span_values,
        attention_mask_matrix,
        attention_lowprec,
        log_partition_sum,
        attention_cotangent,
    )
    kv_grads = jnp.stack(
        [
            grad_kwin.reshape(cluster_rows, key_value_width),
            grad_vwin.reshape(cluster_rows, key_value_width),
        ]
    )
    local_key_value = lax.psum_scatter(
        kv_grads.astype(jnp.bfloat16), "fsdp", scatter_dimension=1, tiled=True
    ).astype(jnp.float32)
    d_query, grad_query_gain = root_mean_square_reverse(
        query_raw,
        inv_query,
        gain_sequence[1],
        rotary_embed_invert(
            query_lowprec_gradient.reshape(local_rows, QUERY_HEADS, HEAD_SIZE),
            rotary_cosine,
            rotary_sine,
        ),
    )
    key_cotangent, key_gain_gradient = root_mean_square_reverse(
        key_unrotated,
        key_inverse_norm,
        gain_sequence[2],
        rotary_embed_invert(
            local_key_value[0].reshape(local_rows, KEY_VALUE_HEADS, HEAD_SIZE),
            rotary_cosine,
            rotary_sine,
        ),
    )
    d_projected = jnp.concatenate(
        [
            d_query.reshape(local_rows, -1),
            key_cotangent.reshape(local_rows, -1),
            local_key_value[1],
        ],
        axis=1,
    ).astype(jnp.bfloat16)
    grad_qkv = tdot(normed_in, d_projected)
    d_normed_in = transposed_product(d_projected, collected_rows[0])
    back_in, grad_attn_gain = root_mean_square_reverse(
        tokens, inv_in, gain_sequence[0], d_normed_in
    )
    grad_tokens = d_mid + back_in
    grads_local = (
        grad_qkv,
        grad_out_proj,
        grad_gate_up,
        grad_down,
        grad_attn_gain,
        grad_query_gain,
        key_gain_gradient,
        grad_ffn_gain,
    )
    grad_share = (
        lax.psum_scatter(
            grads_local[0].astype(jnp.bfloat16), "fsdp", scatter_dimension=0, tiled=True
        ).astype(jnp.float32),
        lax.psum_scatter(
            grads_local[1].astype(jnp.bfloat16), "fsdp", scatter_dimension=0, tiled=True
        ).astype(jnp.float32),
        lax.psum_scatter(
            grads_local[2].astype(jnp.bfloat16), "fsdp", scatter_dimension=0, tiled=True
        ).astype(jnp.float32),
        lax.psum_scatter(
            grads_local[3].astype(jnp.bfloat16), "fsdp", scatter_dimension=0, tiled=True
        ).astype(jnp.float32),
        lax.psum_scatter(
            grads_local[4].astype(jnp.bfloat16), "fsdp", scatter_dimension=0, tiled=True
        ).astype(jnp.float32),
        lax.psum_scatter(
            grads_local[5].astype(jnp.bfloat16), "fsdp", scatter_dimension=0, tiled=True
        ).astype(jnp.float32),
        lax.psum_scatter(
            grads_local[6].astype(jnp.bfloat16), "fsdp", scatter_dimension=0, tiled=True
        ).astype(jnp.float32),
        lax.psum_scatter(
            grads_local[7].astype(jnp.bfloat16), "fsdp", scatter_dimension=0, tiled=True
        ).astype(jnp.float32),
    )
    grad_total = (
        lax.psum(grad_share[0].astype(jnp.bfloat16), "rep").astype(jnp.float32),
        lax.psum(grad_share[1].astype(jnp.bfloat16), "rep").astype(jnp.float32),
        lax.psum(grad_share[2].astype(jnp.bfloat16), "rep").astype(jnp.float32),
        lax.psum(grad_share[3].astype(jnp.bfloat16), "rep").astype(jnp.float32),
        lax.psum(grad_share[4].astype(jnp.bfloat16), "rep").astype(jnp.float32),
        lax.psum(grad_share[5].astype(jnp.bfloat16), "rep").astype(jnp.float32),
        lax.psum(grad_share[6].astype(jnp.bfloat16), "rep").astype(jnp.float32),
        lax.psum(grad_share[7].astype(jnp.bfloat16), "rep").astype(jnp.float32),
    )
    return (
        output,
        grad_tokens,
        grad_total[0],
        grad_total[1],
        grad_total[2],
        grad_total[3],
        grad_total[4],
        grad_total[5],
        grad_total[6],
        grad_total[7],
    )


def solution(mesh):
    placed = (
        P(("rep", "fsdp"), None),
        P(),
        P(("rep", "fsdp"), None),
        P("fsdp", None),
        P("fsdp", None),
        P("fsdp", None),
        P("fsdp", None),
        P("fsdp"),
        P("fsdp"),
        P("fsdp"),
        P("fsdp"),
    )
    return jax.shard_map(
        body,
        mesh=mesh,
        in_specs=placed,
        out_specs=(
            P(("rep", "fsdp"), None),
            P(("rep", "fsdp"), None),
            P("fsdp", None),
            P("fsdp", None),
            P("fsdp", None),
            P("fsdp", None),
            P("fsdp"),
            P("fsdp"),
            P("fsdp"),
            P("fsdp"),
        ),
        check_vma=False,
    )
```

profile of v0, /device:TPU:0, one launch (start us, length us, event | category | flops | bytes accessed | tf_op | source)
XLA Modules:
  0.0 968.5 jit_solution(10914518348454304523)
XLA Ops:
  8.0 13.6 %all-gather = bf16[8,1,128]{2,1,0:T(2,128)(2,1)S(1)} all-gather(bf16[1,1,128]{2,1,0:T(2,128)(2,1)} %bitcast.157), channel_id=1, replica_groups=mesh['rep'=4,'fsdp'=8] {'fsdp'}, dimensions={0}, use_global_device_ids=true | all-gather | bytes 2304 | tf_op jit(solution)/shard_map/all_gather | solution.py:144
  25.3 15.0 %all-reduce.7 = (bf16[64]{0:T(256)(128)(2,1)S(1)}, bf16[64]{0:T(256)(128)(2,1)S(1)}) all-reduce(bf16[64]{0:T(256)(128)(2,1)S(1)} %dynamic-update-slice, bf16[64]{0:T(256)(128)(2,1)S(1)} %dynamic-update-slice.1), channel_id=1, replica_groups=mesh['rep'=4,'fsdp'=8] {'fsdp'}, use_global_device_ids=true, to_apply=%add | all-reduce | flops 128 | bytes 512
  42.8 16.7 %all-gather.8.cloned.1.call-done = bf16[1024,2048]{1,0:T(8,128)(2,1)} async-done(((bf16[128,2048]{1,0:T(8,128)(2,1)}), bf16[1024,2048]{1,0:T(8,128)(2,1)}) %all-gather.8.cloned.1.call-update) | async-done | bytes 4194320 | tf_op jit(solution)/shard_map/all_gather | solution.py:140
  59.5 3.1 fusion.40
  68.1 10.1 %all-gather.1 = bf16[8,1,128]{2,1,0:T(2,128)(2,1)S(1)} all-gather(bf16[1,1,128]{2,1,0:T(2,128)(2,1)S(1)} %bitcast.158), channel_id=1, replica_groups=mesh['rep'=4,'fsdp'=8] {'fsdp'}, dimensions={0}, use_global_device_ids=true | all-gather | bytes 2304 | tf_op jit(solution)/shard_map/all_gather | solution.py:147
  79.7 13.1 %all-gather.10.cloned.1.call-done = bf16[2,1024,512]{2,1,0:T(8,128)(2,1)} async-done(((bf16[2,128,512]{2,1,0:T(8,128)(2,1)}), bf16[2,1024,512]{2,1,0:T(8,128)(2,1)}) %all-gather.10.cloned.1.call-update) | async-done | bytes 2097168 | tf_op jit(solution)/shard_map/all_gather | solution.py:179
  92.8 2.6 fusion.42
  95.5 1.5 copy.97
  98.3 1.5 fusion.5
  99.8 2.0 fusion.3
  101.8 1.3 copy-done
  103.1 2.5 fusion.13
  105.7 17.3 %all-gather.12.cloned.1.call-done = bf16[1024,1024]{1,0:T(8,128)(2,1)} async-done(((bf16[128,1024]{1,0:T(8,128)(2,1)}), bf16[1024,1024]{1,0:T(8,128)(2,1)}) %all-gather.12.cloned.1.call-update) | async-done | bytes 2097168 | tf_op jit(solution)/shard_map/all_gather | solution.py:141
  123.0 2.1 multiply_reduce_fusion.6
  126.3 165.9 %all-gather.14.cloned.1.call-done = bf16[1024,9216]{1,0:T(8,128)(2,1)} async-done(((bf16[128,9216]{1,0:T(8,128)(2,1)}), bf16[1024,9216]{1,0:T(8,128)(2,1)}) %all-gather.14.cloned.1.call-update) | async-done | bytes 18874384 | tf_op jit(solution)/shard_map/all_gather | solution.py:142
  292.2 11.3 %fusion.41 = f32[128,9216]{1,0:T(8,128)} fusion(bf16[1024,9216]{1,0:T(8,128)(2,1)} %all-gather.14.cloned.1.call-done, f32[128,1024]{1,0:T(8,128)S(1)} %get-tuple-element.62, f32[1024]{0:T(1024)S(1)} %bitcast.143, f32[128]{0:T(128)S(1)} %get-tuple-element.58), kind=kOutput, calls=%fused_computation.114 | convolution fusion | flops 2416312320 | bytes 24121856 | tf_op jit(solution)/shard_map/dot_general | solution.py:189
  303.5 79.1 %all-gather.16.cloned.1.call-done = bf16[4608,1024]{1,0:T(8,128)(2,1)} async-done(((bf16[576,1024]{1,0:T(8,128)(2,1)}), bf16[4608,1024]{1,0:T(8,128)(2,1)}) %all-gather.16.cloned.1.call-update) | async-done | bytes 9437200 | tf_op jit(solution)/shard_map/all_gather | solution.py:143
  382.6 8.9 multiply_convert_fusion.1
  391.6 12.6 %multiply_reduce_fusion = (bf16[1024]{0:T(1024)(128)(2,1)}, f32[128]{0:T(128)S(1)}, f32[128,1024]{1,0:T(8,128)S(1)}) fusion(f32[128,1024]{1,0:T(8,128)S(1)} %get-tuple-element.62, f32[128]{0:T(128)S(1)} %copy-done.47, f32[1024]{0:T(1024)S(1)} %bitcast.144, bf16[1024,9216]{1,0:T(8,128)(2,1)} %all-gather.14.cloned.1.call-done, ...), kind=kOutput, calls=%fused_computation.39 | convolution fusion | flops 2421423104 | bytes 22289408 | tf_op jit(solution)/shard_map/dot_general | solution.py:121
  405.2 1.5 convolution_convert_fusion.4
  406.7 1.8 copy.100
  409.7 6.5 bitcast_convert_fusion
  416.3 5.7 fusion.2
  422.0 2.0 copy-done.1
  424.0 2.4 bitcast_convert_fusion.1
  426.4 2.3 copy.108
  428.7 2.3 copy.109
  431.0 3.1 pad_maximum_fusion.1
  434.1 3.1 convolution_convert_fusion.3
  438.7 1.4 mul.516
  441.3 1.4 mul.534
  443.5 2.0 copy.103
  445.5 1.5 mul.520
  447.0 2.1 copy.104
  449.1 1.4 mul.459
  450.5 1.8 copy.112
  452.3 1.4 mul.538
  453.7 1.8 copy.113
  455.5 3.1 fusion.44
  460.5 2.0 copy.105
  462.5 2.0 copy.102
  464.6 2.5 subtract_convert_fusion
  467.0 1.6 reduce-scatter.6.cloned.1.call-done
  468.6 1.7 slice_convert_fusion.1
  470.4 1.8 copy.110
  473.2 1.3 pad_maximum_fusion.8
  478.4 4.4 convolution_convert_fusion.2
  483.8 5.1 convolution_convert_fusion.1
  489.6 10.9 %convolution_convert_fusion = bf16[1024,9216]{1,0:T(8,128)(2,1)} fusion(bf16[128,4608]{1,0:T(8,128)(2,1)} %copy-done.27, bf16[128,4608]{1,0:T(8,128)(2,1)} %copy-done.26, f32[128,1024]{1,0:T(8,128)S(1)} %get-tuple-element.62, f32[1024]{0:T(1024)S(1)} %bitcast.146, f32[128]{0:T(128)S(1)} %copy-done.48), kind=kOutput, calls=%fused_computation | convolution fusion | flops 2430468096 | bytes 21762560 | tf_op jit(solution)/shard_map/dot_general | solution.py:115
  500.8 4.7 reduce-scatter.10.cloned.1.call-done
  505.5 51.2 %reduce-scatter.8.cloned.1.call-done = bf16[128,2048]{1,0:T(8,128)(2,1)} async-done(((bf16[1024,2048]{1,0:T(8,128)(2,1)}), bf16[128,2048]{1,0:T(8,128)(2,1)}) %reduce-scatter.8.cloned.1.call-update) | async-done | bytes 524304 | tf_op jit(solution)/shard_map/reduce_scatter | solution.py:277
  556.7 100.2 %reduce-scatter.14.cloned.1.call-done = bf16[576,1024]{1,0:T(8,128)(2,1)} async-done(((bf16[4608,1024]{1,0:T(8,128)(2,1)}), bf16[576,1024]{1,0:T(8,128)(2,1)}) %reduce-scatter.14.cloned.1.call-update) | async-done | bytes 1179664 | tf_op jit(solution)/shard_map/reduce_scatter | solution.py:286
  657.0 188.6 %reduce-scatter.12.cloned.1.call-done = bf16[128,9216]{1,0:T(8,128)(2,1)} async-done(((bf16[1024,9216]{1,0:T(8,128)(2,1)}), bf16[128,9216]{1,0:T(8,128)(2,1)}) %reduce-scatter.12.cloned.1.call-update) | async-done | bytes 2359312 | tf_op jit(solution)/shard_map/reduce_scatter | solution.py:283
  849.4 1.4 copy.115
  850.9 1.4 copy.116
  852.3 3.3 fusion.15
  855.5 5.9 convolution_add_fusion.1
  862.0 1.4 fusion.17
  863.5 4.0 multiply_reduce_fusion.1
  867.5 14.3 %all-reduce.6 = (bf16[1024]{0:T(1024)(128)(2,1)S(1)}, bf16[64]{0:T(256)(128)(2,1)S(1)}, bf16[64]{0:T(256)(128)(2,1)S(1)}, bf16[1024]{0:T(1024)(128)(2,1)S(1)}) all-reduce(bf16[1024]{0:T(1024)(128)(2,1)S(1)} %get-tuple-element.12, bf16[64]{0:T(256)(128)(2,1)S(1)} %copy-done.56, ...), channel_id=7, replica_groups=mesh['rep'=4,'fsdp'=8] {'fsdp'}, use_global_device_ids=true, to_apply=%region_21.22.clone | all-reduce | flops 2176 | bytes 8704
  882.0 10.3 %all-reduce.8 = (bf16[128]{0:T(256)(128)(2,1)S(1)}, bf16[8]{0:T(256)(128)(2,1)S(1)}, bf16[8]{0:T(256)(128)(2,1)S(1)}, bf16[128]{0:T(256)(128)(2,1)S(1)}) all-reduce(bf16[128]{0:T(256)(128)(2,1)S(1)} %dynamic-slice.3, bf16[8]{0:T(256)(128)(2,1)S(1)} %dynamic-slice.5, ...), channel_id=1, replica_groups=mesh['rep'=4,'fsdp'=8] {'rep'}, use_global_device_ids=true, to_apply=%region_22.23 | all-reduce | flops 272 | bytes 1088 | tf_op jit(solution)/shard_map/psum | solution.py:307
  895.4 58.3 %all-reduce.12.cloned.1.call-done = (bf16[128,2048]{1,0:T(8,128)(2,1)}, bf16[128,1024]{1,0:T(8,128)(2,1)}, bf16[128,9216]{1,0:T(8,128)(2,1)}, bf16[576,1024]{1,0:T(8,128)(2,1)}) async-done(((bf16[128,2048]{1,0:T(8,128)(2,1)}, bf16[128,1024]{1,0:T(8,128)(2,1)}, bf16[128,9216]{1,0:T(8,128)(2,1)}, bf16[576,1024]{1,0:T(8,128)(2,1)}), (bf16[128,2048]{1,0:T(8,128)(2,1)}, bf16[128,1024]{1,0:T(8,128)(2,1)}, ...) | async-done | bytes 4325392 | tf_op jit(solution)/shard_map/psum | solution.py:303
  953.7 4.4 convert_element_type.164
  958.1 1.7 convert_element_type.166
  (217 shorter events, 38.1 us)
Async XLA Ops:
  7.2 52.3 %all-gather.8.cloned.1.call-start = ((), (), s32[]{:S(2)}) async-start(), calls=%async_computation.5 | async-start | bytes 4718592 | tf_op jit(solution)/shard_map/all_gather | solution.py:140
  7.9 84.9 %all-gather.10.cloned.1.call-start = ((), (), s32[]{:S(2)}) async-start(), calls=%async_computation.6 | async-start | bytes 2359296 | tf_op jit(solution)/shard_map/all_gather | solution.py:179
  40.3 26.4 %copy-start.61 = (bf16[64]{0:T(256)(128)(2,1)}, bf16[64]{0:T(256)(128)(2,1)S(1)}, u32[]{:S(2)}) copy-start(bf16[64]{0:T(256)(128)(2,1)S(1)} %get-tuple-element.19) | copy-start | bytes 388
  40.3 23.4 %copy-start.55 = (f32[64]{0:T(128)}, f32[64]{0:T(128)S(1)}, u32[]{:S(2)}) copy-start(f32[64]{0:T(128)S(1)} %convert_element_type.142) | copy-start | bytes 772
  42.6 20.1 %copy-start.50 = (f32[128]{0:T(128)}, f32[128]{0:T(128)S(1)}, u32[]{:S(2)}) copy-start(f32[128]{0:T(128)S(1)} %get-tuple-element.56) | copy-start | bytes 1540
  42.8 36.8 %copy-start.39 = (f32[128,32]{0,1:T(8,128)}, f32[128,32]{0,1:T(8,128)S(1)}, u32[]{:S(2)}) copy-start(f32[128,32]{0,1:T(8,128)S(1)} %get-tuple-element.51) | copy-start | bytes 49156
  42.8 36.8 %copy-start.41 = (f32[128,32]{0,1:T(8,128)}, f32[128,32]{0,1:T(8,128)S(1)}, u32[]{:S(2)}) copy-start(f32[128,32]{0,1:T(8,128)S(1)} %get-tuple-element.52) | copy-start | bytes 49156
  62.6 15.8 %copy-start.8 = (f32[128,2048]{1,0:T(8,128)}, f32[128,2048]{1,0:T(8,128)S(1)}, u32[]{:S(2)}) copy-start(f32[128,2048]{1,0:T(8,128)S(1)} %fusion.40) | copy-start | bytes 3145732
  62.6 5.5 copy-start.59
  62.7 15.5 %copy-start.12 = (f32[128,512]{1,0:T(8,128)}, f32[128,512]{1,0:T(8,128)S(1)}, u32[]{:S(2)}) copy-start(f32[128,512]{1,0:T(8,128)S(1)} %slice.71) | copy-start | bytes 786436
  63.7 4.5 copy-start.44
  64.7 58.3 %all-gather.12.cloned.1.call-start = ((), (), s32[]{:S(2)}) async-start(), calls=%async_computation.7 | async-start | bytes 2359296 | tf_op jit(solution)/shard_map/all_gather | solution.py:141
  65.4 226.8 %all-gather.14.cloned.1.call-start = ((), (), s32[]{:S(2)}) async-start(), calls=%async_computation.8 | async-start | bytes 21233664 | tf_op jit(solution)/shard_map/all_gather | solution.py:142
  66.0 316.6 %all-gather.16.cloned.1.call-start = ((), (), s32[]{:S(2)}) async-start(), calls=%async_computation.9 | async-start | bytes 10616832 | tf_op jit(solution)/shard_map/all_gather | solution.py:143
  66.6 402.0 %reduce-scatter.6.cloned.1.call-start = ((), (), s32[]{:S(2)}) async-start(), calls=%async_computation.10 | async-start | bytes 2359296 | tf_op jit(solution)/shard_map/reduce_scatter | solution.py:229
  66.7 28.8 %copy-start.52 = (f32[64]{0:T(128)}, f32[64]{0:T(128)S(1)}, u32[]{:S(2)}) copy-start(f32[64]{0:T(128)S(1)} %convert_element_type.145) | copy-start | bytes 772
  78.4 23.3 %copy-start.20 = (pred[128,1024]{0,1:T(8,128)(4,1)}, pred[128,1024]{0,1:T(8,128)(4,1)S(1)}, u32[]{:S(2)}) copy-start(pred[128,1024]{0,1:T(8,128)(4,1)S(1)} %fusion.18) | copy-start | bytes 393220
  78.5 17.0 %copy-start.10 = (f32[128,1024]{1,0:T(8,128)}, f32[128,1024]{1,0:T(8,128)S(1)}, u32[]{:S(2)}) copy-start(f32[128,1024]{1,0:T(8,128)S(1)} %slice.77) | copy-start | bytes 1572868
  78.7 18.3 %copy-start.4 = (f32[128,1024]{0,1:T(8,128)}, f32[128,1024]{0,1:T(8,128)S(1)}, u32[]{:S(2)}) copy-start(f32[128,1024]{0,1:T(8,128)S(1)} %copy.98) | copy-start | bytes 1572868
  79.7 18.6 %copy-start.22 = (bf16[128,16,32]{0,2,1:T(8,128)(2,1)}, bf16[128,16,32]{0,2,1:T(8,128)(2,1)S(1)}, u32[]{:S(2)}) copy-start(bf16[128,16,32]{0,2,1:T(8,128)(2,1)S(1)} %get-tuple-element.35) | copy-start | bytes 393220
  79.7 18.6 %copy-start.24 = (bf16[128,16,32]{0,2,1:T(8,128)(2,1)}, bf16[128,16,32]{0,2,1:T(8,128)(2,1)S(1)}, u32[]{:S(2)}) copy-start(bf16[128,16,32]{0,2,1:T(8,128)(2,1)S(1)} %get-tuple-element.36) | copy-start | bytes 393220
  99.8 3.4 copy-start
  99.8 3.4 copy-start.33
  103.1 19.9 %copy-start.2 = (f32[128,1024]{1,0:T(8,128)S(1)}, f32[128,1024]{1,0:T(8,128)}, u32[]{:S(2)}) copy-start(f32[128,1024]{1,0:T(8,128)} %param.11) | copy-start | bytes 1572868
  105.7 197.9 %copy-start.17 = (bf16[8,64,2,128]{3,1,2,0:T(8,128)(2,1)}, bf16[8,64,2,128]{3,1,2,0:T(8,128)(2,1)S(1)}, u32[]{:S(2)}) copy-start(bf16[8,64,2,128]{3,1,2,0:T(8,128)(2,1)S(1)} %fusion.13) | copy-start | bytes 786436
  125.7 177.8 %copy-start.46 = (f32[128]{0:T(128)}, f32[128]{0:T(128)S(1)}, u32[]{:S(2)}) copy-start(f32[128]{0:T(128)S(1)} %get-tuple-element.58) | copy-start | bytes 1540
  382.6 8.9 copy-start.47
  391.5 12.7 %copy-start.26 = (bf16[128,4608]{1,0:T(8,128)(2,1)}, bf16[128,4608]{1,0:T(8,128)(2,1)S(1)}, u32[]{:S(2)}) copy-start(bf16[128,4608]{1,0:T(8,128)(2,1)S(1)} %get-tuple-element.28) | copy-start | bytes 3538948
  391.6 12.7 %copy-start.27 = (bf16[128,4608]{1,0:T(8,128)(2,1)}, bf16[128,4608]{1,0:T(8,128)(2,1)S(1)}, u32[]{:S(2)}) copy-start(bf16[128,4608]{1,0:T(8,128)(2,1)S(1)} %get-tuple-element.29) | copy-start | bytes 3538948
  391.6 12.6 %copy-start.18 = (f32[128,1024]{1,0:T(8,128)S(1)}, f32[128,1024]{1,0:T(8,128)}, u32[]{:S(2)}) copy-start(f32[128,1024]{1,0:T(8,128)} %param.13) | copy-start | bytes 1572868
  391.6 12.6 %copy-start.58 = (f32[128]{0:T(128)S(1)}, f32[128]{0:T(128)}, u32[]{:S(2)}) copy-start(f32[128]{0:T(128)} %get-tuple-element.57) | copy-start | bytes 1540
  391.6 13.6 %copy-start.3 = (bf16[1024,1024]{1,0:T(8,128)(2,1)S(1)}, bf16[1024,1024]{1,0:T(8,128)(2,1)}, u32[]{:S(2)}) copy-start(bf16[1024,1024]{1,0:T(8,128)(2,1)} %all-gather.12.cloned.1.call-done) | copy-start | bytes 6291460
  409.7 6.6 copy-start.21
  409.7 6.6 copy-start.34
  409.7 6.5 copy-start.35
  409.7 6.5 copy-start.49
  416.2 7.8 copy-start.23
  416.3 7.8 copy-start.25
  422.0 2.0 copy-start.1
  434.0 71.5 %reduce-scatter.10.cloned.1.call-start = ((), (), s32[]{:S(2)}) async-start(), calls=%async_computation.12 | async-start | bytes 2359296 | tf_op jit(solution)/shard_map/reduce_scatter | solution.py:280
  437.2 119.5 %reduce-scatter.8.cloned.1.call-start = ((), (), s32[]{:S(2)}) async-start(), calls=%async_computation.11 | async-start | bytes 4718592 | tf_op jit(solution)/shard_map/reduce_scatter | solution.py:277
  455.5 3.1 copy-start.40
  455.5 3.1 copy-start.42
  455.5 3.2 copy-start.5
  455.5 3.2 copy-start.53
  458.6 6.0 copy-start.9
  482.8 174.2 %reduce-scatter.14.cloned.1.call-start = ((), (), s32[]{:S(2)}) async-start(), calls=%async_computation.14 | async-start | bytes 10616832 | tf_op jit(solution)/shard_map/reduce_scatter | solution.py:286
  488.9 356.6 %reduce-scatter.12.cloned.1.call-start = ((), (), s32[]{:S(2)}) async-start(), calls=%async_computation.13 | async-start | bytes 21233664 | tf_op jit(solution)/shard_map/reduce_scatter | solution.py:283
  500.5 346.5 %copy-start.11 = (f32[128,1024]{1,0:T(8,128)S(1)}, f32[128,1024]{1,0:T(8,128)}, u32[]{:S(2)}) copy-start(f32[128,1024]{1,0:T(8,128)} %copy-done.10) | copy-start | bytes 1572868
  500.5 347.7 %copy-start.45 = (f32[128,8]{0,1:T(8,128)S(1)}, f32[128,8]{0,1:T(8,128)}, u32[]{:S(2)}) copy-start(f32[128,8]{0,1:T(8,128)} %copy-done.44) | copy-start | bytes 12292
  500.5 347.8 %copy-start.13 = (f32[128,512]{1,0:T(8,128)S(1)}, f32[128,512]{1,0:T(8,128)}, u32[]{:S(2)}) copy-start(f32[128,512]{1,0:T(8,128)} %copy-done.12) | copy-start | bytes 786436
  500.5 350.4 %copy-start.15 = (f32[128,16,32]{0,2,1:T(8,128)S(1)}, f32[128,16,32]{0,2,1:T(8,128)}, u32[]{:S(2)}) copy-start(f32[128,16,32]{0,2,1:T(8,128)} %copy-done.14) | copy-start | bytes 786436
  500.6 453.1 %all-reduce.12.cloned.1.call-start = ((), (), s32[]{:S(2)}) async-start(), calls=%async_computation.15 | async-start | bytes 8650752 | tf_op jit(solution)/shard_map/psum | solution.py:303
  855.5 5.9 copy-start.32
  855.5 6.2 copy-start.30
  855.5 7.9 copy-start.36
  855.5 7.9 copy-start.51
  861.7 5.7 copy-start.54
  861.7 5.7 copy-start.56
  861.7 32.7 %copy-start.7 = (f32[128,1024]{1,0:T(8,128)S(1)}, f32[128,1024]{1,0:T(8,128)}, u32[]{:S(2)}) copy-start(f32[128,1024]{1,0:T(8,128)} %copy-done.6) | copy-start | bytes 1572868
  861.7 32.7 %copy-start.57 = (f32[128]{0:T(128)S(1)}, f32[128]{0:T(128)}, u32[]{:S(2)}) copy-start(f32[128]{0:T(128)} %get-tuple-element.55) | copy-start | bytes 1540
  953.7 4.5 copy-start.28
  953.7 6.2 copy-start.38
  958.1 2.8 copy-start.43
  (9 other events, 8.3 us)
Sparse Core Ops, SparseCore 0:
  9.6 49.8 all-gather.7
  64.8 27.9 all-gather.9
  94.4 28.5 all-gather.11
  124.5 167.6 all-gather.13
  293.7 88.8 all-gather.15
  434.1 34.4 reduce-scatter.5
  470.9 34.5 reduce-scatter.9
  508.4 48.2 reduce-scatter.7
  559.0 97.8 reduce-scatter.13
  659.2 186.3 reduce-scatter.11
  849.3 104.2 all-reduce.11
where the time goes:
time: 972 us; the launch traced here: 968 us
  waiting for transfers between devices  699 us (72%)
  matrix products  94.7 us (10%)
  blocking collectives  63.3 us (7%)
  local copies, waits for them, and re-layouts  56.8 us (6%)
  other arithmetic  36.6 us (4%)
  between operations  16.9 us (2%)
    reduce_scatter x1, waiting for transfers between devices, body(): lax.psum_scatter(grads_local[2].astype(jnp.bfloat16), 'fsdp', scatter_dim...  189 us
    all_gather x1, waiting for transfers between devices, body(): lax.all_gather(shards[2], 'fsdp', axis=0, tiled=True)  166 us
    reduce_scatter x1, waiting for transfers between devices, body(): lax.psum_scatter(grads_local[3].astype(jnp.bfloat16), 'fsdp', scatter_dim...  100 us
    all_gather x1, waiting for transfers between devices, body(): lax.all_gather(shards[3], 'fsdp', axis=0, tiled=True)  79.1 us
    psum x1, waiting for transfers between devices, body(): lax.psum(grad_share[0].astype(jnp.bfloat16), 'rep').astype(jnp.float32)  58.3 us
    reduce_scatter x1, waiting for transfers between devices, body(): lax.psum_scatter(grads_local[0].astype(jnp.bfloat16), 'fsdp', scatter_dim...  51.2 us
    unnamed x2, blocking collectives  29.3 us
    dot_general x4, matrix products, transposed_product(): lax.dot_general(left_arr, right_arr, (((1,), (1,)), ((), ())), preferred_...  27 us
  transfers between devices with their start and end apart: 11, of which 11 were waited for; matrix products, arithmetic and copies ran while one was open for 12% of the time, Pallas kernels for 0%

commit v1 on v0

--- a/solution.py
+++ b/solution.py
@@ -299,8 +299,9 @@
             grads_local[7].astype(jnp.bfloat16), "fsdp", scatter_dimension=0, tiled=True
         ).astype(jnp.float32),
     )
+    chunk_move = lambda x_in, ax_name: jnp.sum(lax.all_gather(x_in, axis_name=ax_name), axis=0)
     grad_total = (
-        lax.psum(grad_share[0].astype(jnp.bfloat16), "rep").astype(jnp.float32),
+        chunk_move(grad_share[0].astype(jnp.bfloat16), "rep").astype(jnp.float32),
         lax.psum(grad_share[1].astype(jnp.bfloat16), "rep").astype(jnp.float32),
         lax.psum(grad_share[2].astype(jnp.bfloat16), "rep").astype(jnp.float32),
         lax.psum(grad_share[3].astype(jnp.bfloat16), "rep").astype(jnp.float32),

time: 972 us -> 1010 us (1.039)
  waiting for transfers between devices: 699 us -> 735 us
    reduce_scatter x1, waiting for transfers between devices: 4.73 us -> 37 us  [body(): lax.psum_scatter(grads_local[1].astype(jnp.bfloat16), 'fsdp', scatter_dim...]
    reduce_scatter x1, waiting for transfers between devices: 51.2 us -> 27.7 us  [body(): lax.psum_scatter(grads_local[0].astype(jnp.bfloat16), 'fsdp', scatter_dim...]
    psum x1, waiting for transfers between devices: 58.3 us -> 81.8 us  [body(): lax.psum(grad_share[1].astype(jnp.bfloat16), 'rep').astype(jnp.float32)]
  transfers between devices with their start and end apart: 11 -> 12, of which waited for: 11 -> 11; matrix products, arithmetic and copies ran while one was open for 12% -> 11% of each run, Pallas kernels for 0% -> 0%
where the time goes in v1:
time: 1010 us
  waiting for transfers between devices  735 us (73%)
  matrix products  95.2 us (9%)
  blocking collectives  62.6 us (6%)
  local copies, waits for them, and re-layouts  60 us (6%)
  other arithmetic  38 us (4%)
  between operations  17.2 us (2%)
    reduce_scatter x1, waiting for transfers between devices, body(): lax.psum_scatter(grads_local[2].astype(jnp.bfloat16), 'fsdp', scatter_dim...  189 us
    all_gather x1, waiting for transfers between devices, body(): lax.all_gather(shards[2], 'fsdp', axis=0, tiled=True)  166 us
    reduce_scatter x1, waiting for transfers between devices, body(): lax.psum_scatter(grads_local[3].astype(jnp.bfloat16), 'fsdp', scatter_dim...  100 us
    psum x1, waiting for transfers between devices, body(): lax.psum(grad_share[1].astype(jnp.bfloat16), 'rep').astype(jnp.float32)  81.8 us
    all_gather x1, waiting for transfers between devices, body(): lax.all_gather(shards[3], 'fsdp', axis=0, tiled=True)  79.1 us
    reduce_scatter x1, waiting for transfers between devices, body(): lax.psum_scatter(grads_local[1].astype(jnp.bfloat16), 'fsdp', scatter_dim...  37 us
    unnamed x2, blocking collectives  28.9 us
    reduce_scatter x1, waiting for transfers between devices, body(): lax.psum_scatter(grads_local[0].astype(jnp.bfloat16), 'fsdp', scatter_dim...  27.7 us
  transfers between devices with their start and end apart: 12, of which 11 were waited for; matrix products, arithmetic and copies ran while one was open for 11% of the time, Pallas kernels for 0%

profile of v1, /device:TPU:0, one launch (start us, length us, event | category | flops | bytes accessed | tf_op | source)
XLA Modules:
  0.0 1008.9 jit_solution(15651389630529209557)
XLA Ops:
  8.0 13.6 %all-gather.1 = bf16[8,1,128]{2,1,0:T(2,128)(2,1)S(1)} all-gather(bf16[1,1,128]{2,1,0:T(2,128)(2,1)} %bitcast.159), channel_id=1, replica_groups=mesh['rep'=4,'fsdp'=8] {'fsdp'}, dimensions={0}, use_global_device_ids=true | all-gather | bytes 2304 | tf_op jit(solution)/shard_map/all_gather | solution.py:144
  25.3 15.0 %all-reduce.7 = (bf16[64]{0:T(256)(128)(2,1)S(1)}, bf16[64]{0:T(256)(128)(2,1)S(1)}) all-reduce(bf16[64]{0:T(256)(128)(2,1)S(1)} %dynamic-update-slice, bf16[64]{0:T(256)(128)(2,1)S(1)} %dynamic-update-slice.1), channel_id=1, replica_groups=mesh['rep'=4,'fsdp'=8] {'fsdp'}, use_global_device_ids=true, to_apply=%add | all-reduce | flops 128 | bytes 512
  42.8 16.7 %all-gather.10.cloned.1.call-done = bf16[1024,2048]{1,0:T(8,128)(2,1)} async-done(((bf16[128,2048]{1,0:T(8,128)(2,1)}), bf16[1024,2048]{1,0:T(8,128)(2,1)}) %all-gather.10.cloned.1.call-update) | async-done | bytes 4194320 | tf_op jit(solution)/shard_map/all_gather | solution.py:140
  59.5 3.1 fusion.40
  68.2 10.1 all-gather.2
  79.8 13.1 %all-gather.12.cloned.1.call-done = bf16[2,1024,512]{2,1,0:T(8,128)(2,1)} async-done(((bf16[2,128,512]{2,1,0:T(8,128)(2,1)}), bf16[2,1024,512]{2,1,0:T(8,128)(2,1)}) %all-gather.12.cloned.1.call-update) | async-done | bytes 2097168 | tf_op jit(solution)/shard_map/all_gather | solution.py:179
  92.8 2.6 fusion.42
  95.5 1.5 copy.97
  98.3 1.5 fusion.5
  99.8 2.0 fusion.3
  103.1 2.5 fusion.13
  105.7 17.3 %all-gather.14.cloned.1.call-done = bf16[1024,1024]{1,0:T(8,128)(2,1)} async-done(((bf16[128,1024]{1,0:T(8,128)(2,1)}), bf16[1024,1024]{1,0:T(8,128)(2,1)}) %all-gather.14.cloned.1.call-update) | async-done | bytes 2097168 | tf_op jit(solution)/shard_map/all_gather | solution.py:141
  123.0 2.1 multiply_reduce_fusion.6
  126.3 165.9 %all-gather.16.cloned.1.call-done = bf16[1024,9216]{1,0:T(8,128)(2,1)} async-done(((bf16[128,9216]{1,0:T(8,128)(2,1)}), bf16[1024,9216]{1,0:T(8,128)(2,1)}) %all-gather.16.cloned.1.call-update) | async-done | bytes 18874384 | tf_op jit(solution)/shard_map/all_gather | solution.py:142
  292.2 11.3 %fusion.41 = f32[128,9216]{1,0:T(8,128)} fusion(bf16[1024,9216]{1,0:T(8,128)(2,1)} %all-gather.16.cloned.1.call-done, f32[128,1024]{1,0:T(8,128)S(1)} %get-tuple-element.61, f32[1024]{0:T(1024)S(1)} %bitcast.145, f32[128]{0:T(128)S(1)} %get-tuple-element.57), kind=kOutput, calls=%fused_computation.114 | convolution fusion | flops 2416312320 | bytes 24121856 | tf_op jit(solution)/shard_map/dot_general | solution.py:189
  303.5 79.1 %all-gather.18.cloned.1.call-done = bf16[4608,1024]{1,0:T(8,128)(2,1)} async-done(((bf16[576,1024]{1,0:T(8,128)(2,1)}), bf16[4608,1024]{1,0:T(8,128)(2,1)}) %all-gather.18.cloned.1.call-update) | async-done | bytes 9437200 | tf_op jit(solution)/shard_map/all_gather | solution.py:143
  382.6 8.9 multiply_convert_fusion.1
  391.6 12.6 %multiply_reduce_fusion = (bf16[1024]{0:T(1024)(128)(2,1)}, f32[128]{0:T(128)S(1)}, f32[128,1024]{1,0:T(8,128)S(1)}) fusion(f32[128,1024]{1,0:T(8,128)S(1)} %get-tuple-element.61, f32[128]{0:T(128)S(1)} %copy-done.44, f32[1024]{0:T(1024)S(1)} %bitcast.146, bf16[1024,9216]{1,0:T(8,128)(2,1)} %all-gather.16.cloned.1.call-done, ...), kind=kOutput, calls=%fused_computation.39 | convolution fusion | flops 2421423104 | bytes 22289408 | tf_op jit(solution)/shard_map/dot_general | solution.py:121
  405.3 1.5 convolution_convert_fusion.4
  406.8 1.8 copy.100
  409.8 6.5 bitcast_convert_fusion
  416.3 5.7 fusion.2
  422.1 2.0 copy-done.1
  424.1 2.4 bitcast_convert_fusion.1
  426.4 2.3 copy.108
  428.7 2.3 copy.109
  431.0 3.1 pad_maximum_fusion.1
  435.5 1.4 mul.516
  438.1 1.3 mul.534
  440.3 2.0 copy.103
  442.4 1.5 mul.520
  443.9 2.1 copy.104
  445.9 1.4 mul.459
  447.3 1.8 copy.112
  449.1 1.4 mul.538
  450.5 1.8 copy.113
  452.3 3.1 fusion.44
  457.3 2.0 copy.105
  459.4 2.0 copy.102
  461.4 2.5 subtract_convert_fusion
  463.9 4.8 reduce-scatter.6.cloned.1.call-done
  468.7 1.7 slice_convert_fusion.1
  470.4 1.8 copy.110
  473.2 1.4 pad_maximum_fusion.8
  478.5 4.4 convolution_convert_fusion.2
  484.0 2.0 convolution_convert_fusion.3
  486.1 6.1 convolution_convert_fusion.1
  492.9 11.0 %convolution_convert_fusion = bf16[1024,9216]{1,0:T(8,128)(2,1)} fusion(bf16[128,4608]{1,0:T(8,128)(2,1)} %copy-done.26, bf16[128,4608]{1,0:T(8,128)(2,1)} %copy-done.25, f32[128,1024]{1,0:T(8,128)S(1)} %get-tuple-element.61, f32[1024]{0:T(1024)S(1)} %bitcast.148, f32[128]{0:T(128)S(1)} %copy-done.45), kind=kOutput, calls=%fused_computation | convolution fusion | flops 2430468096 | bytes 21762560 | tf_op jit(solution)/shard_map/dot_general | solution.py:115
  503.9 27.7 %reduce-scatter.8.cloned.1.call-done = bf16[128,2048]{1,0:T(8,128)(2,1)} async-done(((bf16[1024,2048]{1,0:T(8,128)(2,1)}), bf16[128,2048]{1,0:T(8,128)(2,1)}) %reduce-scatter.8.cloned.1.call-update) | async-done | bytes 524304 | tf_op jit(solution)/shard_map/reduce_scatter | solution.py:277
  531.9 37.0 %reduce-scatter.10.cloned.1.call-done = bf16[128,1024]{1,0:T(8,128)(2,1)} async-done(((bf16[1024,1024]{1,0:T(8,128)(2,1)}), bf16[128,1024]{1,0:T(8,128)(2,1)}) %reduce-scatter.10.cloned.1.call-update) | async-done | bytes 262160 | tf_op jit(solution)/shard_map/reduce_scatter | solution.py:280
  568.9 100.5 %reduce-scatter.14.cloned.1.call-done = bf16[576,1024]{1,0:T(8,128)(2,1)} async-done(((bf16[4608,1024]{1,0:T(8,128)(2,1)}), bf16[576,1024]{1,0:T(8,128)(2,1)}) %reduce-scatter.14.cloned.1.call-update) | async-done | bytes 1179664 | tf_op jit(solution)/shard_map/reduce_scatter | solution.py:286
  669.3 188.6 %reduce-scatter.12.cloned.1.call-done = bf16[128,9216]{1,0:T(8,128)(2,1)} async-done(((bf16[1024,9216]{1,0:T(8,128)(2,1)}), bf16[128,9216]{1,0:T(8,128)(2,1)}) %reduce-scatter.12.cloned.1.call-update) | async-done | bytes 2359312 | tf_op jit(solution)/shard_map/reduce_scatter | solution.py:283
  863.3 2.3 copy.115
  865.6 2.3 copy.116
  867.9 2.5 fusion.15
  870.4 5.9 convolution_add_fusion.1
  876.8 1.4 fusion.17
  878.2 4.4 multiply_reduce_fusion.1
  882.7 13.9 %all-reduce.6 = (bf16[1024]{0:T(1024)(128)(2,1)S(1)}, bf16[64]{0:T(256)(128)(2,1)S(1)}, bf16[64]{0:T(256)(128)(2,1)S(1)}, bf16[1024]{0:T(1024)(128)(2,1)S(1)}) all-reduce(bf16[1024]{0:T(1024)(128)(2,1)S(1)} %get-tuple-element.12, bf16[64]{0:T(256)(128)(2,1)S(1)} %fusion.15, ...), channel_id=8, replica_groups=mesh['rep'=4,'fsdp'=8] {'fsdp'}, use_global_device_ids=true, to_apply=%region_21.22.clone | all-reduce | flops 2176 | bytes 8704
  896.9 10.0 all-reduce.8
  909.9 2.0 reduce_sum.148
  913.0 81.8 %all-reduce.12.cloned.1.call-done = (bf16[128,1024]{1,0:T(8,128)(2,1)}, bf16[128,9216]{1,0:T(8,128)(2,1)}, bf16[576,1024]{1,0:T(8,128)(2,1)}) async-done(((bf16[128,1024]{1,0:T(8,128)(2,1)}, bf16[128,9216]{1,0:T(8,128)(2,1)}, bf16[576,1024]{1,0:T(8,128)(2,1)}), (bf16[128,1024]{1,0:T(8,128)(2,1)}, bf16[128,9216]{1,0:T(8,128)(2,1)}, bf16[576,1024]{1,0:T(8,128)(2,1)})) %all-reduce.12.cloned.1.call-update) | async-done | bytes 3801104 | tf_op jit(solution)/shard_map/psum | solution.py:305
  994.8 4.4 convert_element_type.166
  999.2 1.7 convert_element_type.168
  (213 shorter events, 41.0 us)
Async XLA Ops:
  7.2 52.3 %all-gather.10.cloned.1.call-start = ((), (), s32[]{:S(2)}) async-start(), calls=%async_computation.5 | async-start | bytes 4718592 | tf_op jit(solution)/shard_map/all_gather | solution.py:140
  7.9 84.9 %all-gather.12.cloned.1.call-start = ((), (), s32[]{:S(2)}) async-start(), calls=%async_computation.6 | async-start | bytes 2359296 | tf_op jit(solution)/shard_map/all_gather | solution.py:179
  40.3 26.4 %copy-start.57 = (bf16[64]{0:T(256)(128)(2,1)}, bf16[64]{0:T(256)(128)(2,1)S(1)}, u32[]{:S(2)}) copy-start(bf16[64]{0:T(256)(128)(2,1)S(1)} %get-tuple-element.19) | copy-start | bytes 388
  40.3 23.4 %copy-start.52 = (f32[64]{0:T(128)}, f32[64]{0:T(128)S(1)}, u32[]{:S(2)}) copy-start(f32[64]{0:T(128)S(1)} %convert_element_type.144) | copy-start | bytes 772
  42.6 20.1 %copy-start.47 = (f32[128]{0:T(128)}, f32[128]{0:T(128)S(1)}, u32[]{:S(2)}) copy-start(f32[128]{0:T(128)S(1)} %get-tuple-element.55) | copy-start | bytes 1540
  42.8 36.9 %copy-start.36 = (f32[128,32]{0,1:T(8,128)}, f32[128,32]{0,1:T(8,128)S(1)}, u32[]{:S(2)}) copy-start(f32[128,32]{0,1:T(8,128)S(1)} %get-tuple-element.50) | copy-start | bytes 49156
  42.8 36.9 %copy-start.38 = (f32[128,32]{0,1:T(8,128)}, f32[128,32]{0,1:T(8,128)S(1)}, u32[]{:S(2)}) copy-start(f32[128,32]{0,1:T(8,128)S(1)} %get-tuple-element.51) | copy-start | bytes 49156
  62.6 15.8 %copy-start.8 = (f32[128,2048]{1,0:T(8,128)}, f32[128,2048]{1,0:T(8,128)S(1)}, u32[]{:S(2)}) copy-start(f32[128,2048]{1,0:T(8,128)S(1)} %fusion.40) | copy-start | bytes 3145732
  62.6 5.5 copy-start.55
  62.7 15.5 %copy-start.12 = (f32[128,512]{1,0:T(8,128)}, f32[128,512]{1,0:T(8,128)S(1)}, u32[]{:S(2)}) copy-start(f32[128,512]{1,0:T(8,128)S(1)} %slice.71) | copy-start | bytes 786436
  63.7 4.5 copy-start.41
  64.7 58.3 %all-gather.14.cloned.1.call-start = ((), (), s32[]{:S(2)}) async-start(), calls=%async_computation.7 | async-start | bytes 2359296 | tf_op jit(solution)/shard_map/all_gather | solution.py:141
  65.4 226.8 %all-gather.16.cloned.1.call-start = ((), (), s32[]{:S(2)}) async-start(), calls=%async_computation.8 | async-start | bytes 21233664 | tf_op jit(solution)/shard_map/all_gather | solution.py:142
  66.0 316.6 %all-gather.18.cloned.1.call-start = ((), (), s32[]{:S(2)}) async-start(), calls=%async_computation.9 | async-start | bytes 10616832 | tf_op jit(solution)/shard_map/all_gather | solution.py:143
  66.6 402.1 %reduce-scatter.6.cloned.1.call-start = ((), (), s32[]{:S(2)}) async-start(), calls=%async_computation.10 | async-start | bytes 2359296 | tf_op jit(solution)/shard_map/reduce_scatter | solution.py:229
  66.7 28.8 %copy-start.49 = (f32[64]{0:T(128)}, f32[64]{0:T(128)S(1)}, u32[]{:S(2)}) copy-start(f32[64]{0:T(128)S(1)} %convert_element_type.147) | copy-start | bytes 772
  78.5 23.3 %copy-start.19 = (pred[128,1024]{0,1:T(8,128)(4,1)}, pred[128,1024]{0,1:T(8,128)(4,1)S(1)}, u32[]{:S(2)}) copy-start(pred[128,1024]{0,1:T(8,128)(4,1)S(1)} %fusion.18) | copy-start | bytes 393220
  78.5 17.0 %copy-start.10 = (f32[128,1024]{1,0:T(8,128)}, f32[128,1024]{1,0:T(8,128)S(1)}, u32[]{:S(2)}) copy-start(f32[128,1024]{1,0:T(8,128)S(1)} %slice.77) | copy-start | bytes 1572868
  78.7 18.3 %copy-start.4 = (f32[128,1024]{0,1:T(8,128)}, f32[128,1024]{0,1:T(8,128)S(1)}, u32[]{:S(2)}) copy-start(f32[128,1024]{0,1:T(8,128)S(1)} %copy.98) | copy-start | bytes 1572868
  79.7 18.6 %copy-start.21 = (bf16[128,16,32]{0,2,1:T(8,128)(2,1)}, bf16[128,16,32]{0,2,1:T(8,128)(2,1)S(1)}, u32[]{:S(2)}) copy-start(bf16[128,16,32]{0,2,1:T(8,128)(2,1)S(1)} %get-tuple-element.34) | copy-start | bytes 393220
  79.7 18.6 %copy-start.23 = (bf16[128,16,32]{0,2,1:T(8,128)(2,1)}, bf16[128,16,32]{0,2,1:T(8,128)(2,1)S(1)}, u32[]{:S(2)}) copy-start(bf16[128,16,32]{0,2,1:T(8,128)(2,1)S(1)} %get-tuple-element.35) | copy-start | bytes 393220
  99.8 3.4 copy-start
  99.8 3.4 copy-start.32
  103.1 19.9 %copy-start.2 = (f32[128,1024]{1,0:T(8,128)S(1)}, f32[128,1024]{1,0:T(8,128)}, u32[]{:S(2)}) copy-start(f32[128,1024]{1,0:T(8,128)} %param.11) | copy-start | bytes 1572868
  105.7 197.9 %copy-start.16 = (bf16[8,64,2,128]{3,1,2,0:T(8,128)(2,1)}, bf16[8,64,2,128]{3,1,2,0:T(8,128)(2,1)S(1)}, u32[]{:S(2)}) copy-start(bf16[8,64,2,128]{3,1,2,0:T(8,128)(2,1)S(1)} %fusion.13) | copy-start | bytes 786436
  125.7 177.8 %copy-start.43 = (f32[128]{0:T(128)}, f32[128]{0:T(128)S(1)}, u32[]{:S(2)}) copy-start(f32[128]{0:T(128)S(1)} %get-tuple-element.57) | copy-start | bytes 1540
  382.6 8.9 copy-start.44
  391.5 12.7 %copy-start.25 = (bf16[128,4608]{1,0:T(8,128)(2,1)}, bf16[128,4608]{1,0:T(8,128)(2,1)S(1)}, u32[]{:S(2)}) copy-start(bf16[128,4608]{1,0:T(8,128)(2,1)S(1)} %get-tuple-element.27) | copy-start | bytes 3538948
  391.6 12.7 %copy-start.26 = (bf16[128,4608]{1,0:T(8,128)(2,1)}, bf16[128,4608]{1,0:T(8,128)(2,1)S(1)}, u32[]{:S(2)}) copy-start(bf16[128,4608]{1,0:T(8,128)(2,1)S(1)} %get-tuple-element.28) | copy-start | bytes 3538948
  391.6 12.7 %copy-start.18 = (f32[128,1024]{1,0:T(8,128)S(1)}, f32[128,1024]{1,0:T(8,128)}, u32[]{:S(2)}) copy-start(f32[128,1024]{1,0:T(8,128)} %param.13) | copy-start | bytes 1572868
  391.6 12.7 %copy-start.54 = (f32[128]{0:T(128)S(1)}, f32[128]{0:T(128)}, u32[]{:S(2)}) copy-start(f32[128]{0:T(128)} %get-tuple-element.56) | copy-start | bytes 1540
  391.6 13.7 %copy-start.3 = (bf16[1024,1024]{1,0:T(8,128)(2,1)S(1)}, bf16[1024,1024]{1,0:T(8,128)(2,1)}, u32[]{:S(2)}) copy-start(bf16[1024,1024]{1,0:T(8,128)(2,1)} %all-gather.14.cloned.1.call-done) | copy-start | bytes 6291460
  409.7 6.6 copy-start.20
  409.7 6.6 copy-start.33
  409.7 6.5 copy-start.34
  409.7 6.5 copy-start.46
  416.3 7.8 copy-start.22
  416.3 7.8 copy-start.24
  422.1 2.0 copy-start.1
  434.1 97.5 %reduce-scatter.8.cloned.1.call-start = ((), (), s32[]{:S(2)}) async-start(), calls=%async_computation.11 | async-start | bytes 4718592 | tf_op jit(solution)/shard_map/reduce_scatter | solution.py:277
  452.3 3.1 copy-start.37
  452.3 3.1 copy-start.39
  452.3 3.2 copy-start.5
  452.3 3.2 copy-start.50
  455.4 6.0 copy-start.9
  473.2 1.4 copy-start.28
  473.2 1.4 copy-start.30
  482.9 1.0 copy-start.7
  482.9 1.1 copy-start.17
  482.9 86.0 %reduce-scatter.10.cloned.1.call-start = ((), (), s32[]{:S(2)}) async-start(), calls=%async_computation.12 | async-start | bytes 2359296 | tf_op jit(solution)/shard_map/reduce_scatter | solution.py:280
  486.0 183.3 %reduce-scatter.14.cloned.1.call-start = ((), (), s32[]{:S(2)}) async-start(), calls=%async_computation.14 | async-start | bytes 10616832 | tf_op jit(solution)/shard_map/reduce_scatter | solution.py:286
  492.2 365.7 %reduce-scatter.12.cloned.1.call-start = ((), (), s32[]{:S(2)}) async-start(), calls=%async_computation.13 | async-start | bytes 21233664 | tf_op jit(solution)/shard_map/reduce_scatter | solution.py:283
  503.9 356.1 %copy-start.11 = (f32[128,1024]{1,0:T(8,128)S(1)}, f32[128,1024]{1,0:T(8,128)}, u32[]{:S(2)}) copy-start(f32[128,1024]{1,0:T(8,128)} %copy-done.10) | copy-start | bytes 1572868
  503.9 357.4 %copy-start.42 = (f32[128,8]{0,1:T(8,128)S(1)}, f32[128,8]{0,1:T(8,128)}, u32[]{:S(2)}) copy-start(f32[128,8]{0,1:T(8,128)} %copy-done.41) | copy-start | bytes 12292
  503.9 357.4 %copy-start.13 = (f32[128,512]{1,0:T(8,128)S(1)}, f32[128,512]{1,0:T(8,128)}, u32[]{:S(2)}) copy-start(f32[128,512]{1,0:T(8,128)} %copy-done.12) | copy-start | bytes 786436
  503.9 406.0 %all-gather.20.cloned.1.call-start = ((), (), s32[]{:S(2)}) async-start(), calls=%async_computation.15 | async-start | bytes 2621440 | tf_op jit(solution)/shard_map/all_gather | solution.py:302
  531.6 463.2 %all-reduce.12.cloned.1.call-start = ((), (), s32[]{:S(2)}) async-start(), calls=%async_computation.16 | async-start | bytes 7602176 | tf_op jit(solution)/shard_map/psum | solution.py:305
  870.4 5.9 copy-start.31
  870.4 6.2 copy-start.29
  870.4 7.8 copy-start.48
  876.6 6.1 copy-start.51
  876.6 32.4 %copy-start.53 = (f32[128]{0:T(128)S(1)}, f32[128]{0:T(128)}, u32[]{:S(2)}) copy-start(f32[128]{0:T(128)} %get-tuple-element.54) | copy-start | bytes 1540
  994.8 4.4 copy-start.27
  994.8 6.1 copy-start.40
  (6 other events, 4.5 us)
Sparse Core Ops, SparseCore 0:
  9.6 49.8 all-gather.9
  64.8 27.9 all-gather.11
  94.4 28.5 all-gather.13
  124.5 167.6 all-gather.15
  293.7 88.8 all-gather.17
  434.2 34.4 reduce-scatter.5
  483.0 48.5 reduce-scatter.7
  534.5 34.3 reduce-scatter.9
  571.2 98.1 reduce-scatter.13
  671.5 186.3 reduce-scatter.11
  859.8 33.6 all-gather.19
  896.7 98.0 all-reduce.11
